TPU v7x, 128 devices: a whole 4x4x4 slice. The times are simulated.
128 devices in a mesh: video: 32 (over z_hi, x, y), head: 4 (over z_lo, core).
Axes of the slice: x: 4, y: 4, z: 4 (z_hi: 2, z_lo: 2; z = z_hi * 2 + z_lo), core: 2. Of those that a mesh axis runs over, the one named last changes fastest.
Arguments:
- text_queries: bfloat16 [512, 8192], P('video', 'head'), may hold values from -140 to 140
- visual_keys: bfloat16 [16384, 1024], P('video', 'head'), may hold values from -5 to 5
- visual_values: bfloat16 [16384, 1024], P('video', 'head'), may hold values from -6 to 6
- out_grad: bfloat16 [512, 8192], P('video', 'head'), may hold values from -1536 to 1536
- query_frame: int32 [512], replicated, may hold values from 0 to 15
- block_frame: int32 [128], replicated, may hold values from 0 to 16, as said below
- q_weight: bfloat16 [8192, 8192], P('head', 'video'), may hold values from -0.0625 to 0.0625
Outputs:
- query_grad: bfloat16 [512, 8192], P('video', 'head')
- key_grad: bfloat16 [16384, 1024], P('video', 'head')
- value_grad: bfloat16 [16384, 1024], P('video', 'head')
- text_grad: bfloat16 [512, 8192], P('head', 'video')
Inputs may be any that keep to these rules, and one draw needn't show every extreme that they name: `block_frame`: on each index of video the first 1 to 4 block slots are live and the rest empty; some index has all 4 live. Live blocks carry frame numbers that never fall along the whole array and start at 0; empty slots carry 16.
All inputs are finite; a program needn't handle non-finite values.
Results may differ from a plain program's by a relative error of at most 0.0058.
Values may be sent and summed in bfloat16 or wider, within the bound.
No kernel may reach another device: no remote copies, remote signals or barrier semaphores. Data moves between devices by JAX's collectives and lax.ppermute only.
A program may use at most 384 MiB of HBM per device.

v0:
```python
import jax
import jax.numpy as jnp
from jax import lax
from jax.sharding import Mesh
from jax.sharding import PartitionSpec as P

HEADS = 64
KV_HEADS = 8
HEAD_DIM = 128
BLOCK = 128
VIDEO = ("video_0", "video_1", "video_2")
neg_fill = -1e30


def side_by_side(arrays, axis, dim, along):
    both = jnp.concatenate(arrays, axis=along)
    filled, at, outs = (lax.all_gather(both, axis, axis=dim, tiled=True), 0, [])
    for a in arrays:
        outs.append(lax.slice_in_dim(filled, at, at + a.shape[along], axis=along))
        at += a.shape[along]
    return tuple(outs)


def joined_all(x, axes, combine):
    for axis in axes:
        pieces = jax.tree.map(lambda part: lax.all_gather(part, axis), x)
        x = jax.tree.map(lambda part: part[0], pieces)
        for k in range(1, lax.axis_size(axis)):
            x = combine(x, jax.tree.map(lambda part: part[k], pieces))
    return x


def split_queries(source):
    return source.reshape(source.shape[0], -1, HEADS // KV_HEADS, HEAD_DIM)


def row_frames(block_frame, row_start, piece_rows):
    row_index = row_start + jnp.arange(piece_rows, dtype=jnp.int32)
    return jnp.take(block_frame, row_index // BLOCK)


def key_layout(key_piece, value_piece, frame_rows):
    piece_rows = key_piece.shape[0]
    block_rows = BLOCK
    block_count = piece_rows // block_rows
    local_heads = key_piece.shape[1] // HEAD_DIM
    shaped_keys = key_piece.reshape(block_count, block_rows, local_heads, HEAD_DIM)
    shaped_values = value_piece.reshape(block_count, block_rows, local_heads, HEAD_DIM)
    return (shaped_keys, shaped_values, frame_rows.reshape(block_count, block_rows))


def masked_scores(query_heads, query_limit, key_block, frame_block):
    scores = jnp.einsum(
        "rgjd,kgd->rgjk", query_heads, key_block, preferred_element_type=jnp.float32
    ) * HEAD_DIM ** (-0.5)
    visible = (frame_block[None, :] <= query_limit[:, None])[:, None, None, :]
    return (jnp.where(visible, scores, neg_fill), visible)


def sweep(block_step, running, layout, grads_in):
    shaped_keys, shaped_values, shaped_frames = layout

    def visit_block(state_now, block_items):
        key_block, value_block, frame_block, grads_block = block_items
        return block_step(state_now, key_block, value_block, frame_block, grads_block)

    return lax.scan(visit_block, running, (shaped_keys, shaped_values, shaped_frames, grads_in))


def forward_step(query_heads, query_limit):

    def block_step(running, key_block, value_block, frame_block, grads_in):
        peaks, totals, weighted = running
        scores, visible = masked_scores(query_heads, query_limit, key_block, frame_block)
        new_peak = jnp.maximum(peaks, jnp.max(scores, axis=-1))
        rescale = jnp.exp(peaks - new_peak)
        weights = jnp.where(visible, jnp.exp(scores - new_peak[..., None]), 0.0)
        totals = totals * rescale + jnp.sum(weights, axis=-1)
        weighted = weighted * rescale[..., None] + jnp.einsum(
            "rgjk,kgd->rgjd",
            weights,
            value_block.astype(jnp.float32),
            precision=lax.Precision.HIGHEST,
        )
        return ((new_peak, totals, weighted), grads_in)

    return block_step


def backward_step(query_heads, grad_heads, query_limit, log_total, row_dots):

    def block_step(running, key_block, value_block, frame_block, grads_in):
        scores, visible = masked_scores(query_heads, query_limit, key_block, frame_block)
        weights = jnp.where(visible, jnp.exp(scores - log_total[..., None]), 0.0)
        value_dots = jnp.einsum(
            "rgjd,kgd->rgjk", grad_heads, value_block, preferred_element_type=jnp.float32
        )
        score_grads = (weights * (value_dots - row_dots[..., None])).astype(jnp.bfloat16)
        running = running + jnp.einsum(
            "rgjk,kgd->rgjd", score_grads, key_block, preferred_element_type=jnp.float32
        ) * HEAD_DIM ** (-0.5)
        weight_half = weights.astype(jnp.bfloat16)
        key_part = jnp.einsum(
            "rgjk,rgjd->kgd", score_grads, query_heads, preferred_element_type=jnp.float32
        ) * HEAD_DIM ** (-0.5)
        value_part = jnp.einsum(
            "rgjk,rgjd->kgd", weight_half, grad_heads, preferred_element_type=jnp.float32
        )
        grads_in = (grads_in[0] + key_part, grads_in[1] + value_part)
        return (running, grads_in)

    return block_step


def initial_state(total_rows, local_heads):
    group_size = HEADS // KV_HEADS
    return (
        jnp.full((total_rows, local_heads, group_size), neg_fill, jnp.float32),
        jnp.zeros((total_rows, local_heads, group_size), jnp.float32),
        jnp.zeros((total_rows, local_heads, group_size, HEAD_DIM), jnp.float32),
    )


def combine_parts(earlier, later):
    new_peak = jnp.maximum(earlier[0], later[0])
    early_scale = jnp.exp(earlier[0] - new_peak)
    late_scale = jnp.exp(later[0] - new_peak)
    totals = earlier[1] * early_scale + later[1] * late_scale
    weighted = earlier[2] * early_scale[..., None] + later[2] * late_scale[..., None]
    return (new_peak, totals, weighted)


def shards(text_queries, visual_keys, visual_values, out_grad, query_frame, block_frame, q_weight):
    query_rows = text_queries.shape[0]
    key_rows = visual_keys.shape[0]
    local_heads = visual_keys.shape[1] // HEAD_DIM
    video_index = lax.axis_index(VIDEO)
    own_frames = row_frames(block_frame, video_index * key_rows, key_rows)
    own_layout = key_layout(visual_keys, visual_values, own_frames)
    grad_shape = own_layout[0].shape[:2] + (local_heads, HEAD_DIM)
    all_queries, all_grads = side_by_side((text_queries, out_grad), VIDEO, 0, 1)
    total_rows = all_queries.shape[0]
    query_heads = split_queries(all_queries)
    grad_heads = split_queries(all_grads)
    partial_value, unused = sweep(
        forward_step(query_heads, query_frame),
        initial_state(total_rows, local_heads),
        own_layout,
        (),
    )
    peaks, totals, weighted = joined_all(partial_value, VIDEO, combine_parts)
    row_dots = jnp.sum(grad_heads * (weighted / totals[..., None]), axis=-1)
    log_total = peaks + jnp.log(totals)
    zero_grads = (jnp.zeros(grad_shape, jnp.float32), jnp.zeros(grad_shape, jnp.float32))
    query_start = jnp.zeros(partial_value[2].shape, jnp.float32)
    block_step = backward_step(query_heads, grad_heads, query_frame, log_total, row_dots)
    query_sum, key_value = sweep(block_step, query_start, own_layout, zero_grads)
    query_total = lax.psum(query_sum, VIDEO)
    query_grad_all = query_total.reshape(total_rows, -1).astype(jnp.bfloat16)
    query_grad = lax.dynamic_slice_in_dim(query_grad_all, video_index * query_rows, query_rows, 0)
    key_sum, value_sum = key_value
    key_grad = key_sum.reshape(key_rows, -1).astype(jnp.bfloat16)
    value_grad = value_sum.reshape(key_rows, -1).astype(jnp.bfloat16)
    partial_text = jnp.dot(query_grad_all, q_weight, preferred_element_type=jnp.float32)
    text_grad = lax.psum_scatter(partial_text, "head", scatter_dimension=0, tiled=True).astype(
        jnp.bfloat16
    )
    return (query_grad, key_grad, value_grad, text_grad)


def solution(mesh):
    split = Mesh(
        mesh.devices.reshape(2, 4, 4, mesh.shape["head"]), ("video_0", "video_1", "video_2", "head")
    )
    placed = (
        P(VIDEO, "head"),
        P(VIDEO, "head"),
        P(VIDEO, "head"),
        P(VIDEO, "head"),
        P(),
        P(),
        P("head", VIDEO),
    )
    return jax.shard_map(
        shards,
        mesh=split,
        in_specs=placed,
        out_specs=(P(VIDEO, "head"), P(VIDEO, "head"), P(VIDEO, "head"), P("head", VIDEO)),
        check_vma=False,
    )
```

profile of v0, /device:TPU:1, one launch (start us, length us, event | category | flops | bytes accessed | tf_op | source)
XLA Modules:
  0.0 959.7 jit_solution(10768328933219193713)
XLA Ops:
  15.9 79.9 %all-gather.8.cloned.1.call-done = bf16[512,4096]{1,0:T(8,128)(2,1)} async-done(((bf16[16,4096]{1,0:T(8,128)(2,1)}), bf16[512,4096]{1,0:T(8,128)(2,1)}) %all-gather.8.cloned.1.call-update) | async-done | bytes 4194320 | tf_op jit(solution)/shard_map/all_gather | solution.py:17
  95.8 4.2 fusion.98
  105.6 67.9 %while.30 = (s32[]{:T(128)}, f32[512,2,8]{0,2,1:T(8,128)S(1)}, f32[512,2,8]{0,2,1:T(8,128)S(1)}, f32[512,2,8,128]{0,3,2,1:T(8,128)}, s32[4,128]{1,0:T(4,128)S(1)...) while((s32[]{:T(128)}, f32[512,2,8]{0,2,1:T(8,128)S(1)}, ...), condition=%wide.region_3.4_spmd.clone, body=%wide.region_0.0_spmd.clone.sunk | while | flops 1894883328 | bytes 24252544 | solution.py:67
  113.7 7.9 bitcast_add_fusion.4
  129.7 9.2 bitcast_add_fusion.4
  147.0 9.2 bitcast_add_fusion.4
  164.3 9.2 bitcast_add_fusion.4
  173.5 5.5 copy.70
  179.0 4.9 all-gather
  186.0 99.7 %all-gather.14.cloned.1.call-done = f32[1024,2,8,128]{3,2,1,0:T(8,128)} async-done(((f32[512,2,8,128]{3,2,1,0:T(8,128)}), f32[1024,2,8,128]{3,2,1,0:T(8,128)}) %all-gather.14.cloned.1.call-update) | async-done | bytes 8388624 | tf_op jit(solution)/shard_map/all_gather | solution.py:26
  285.7 8.0 fusion.53
  293.8 4.9 all-gather.1
  299.4 9.4 all_gather.48
  314.9 132.3 %all-gather.10.cloned.1.call-done = f32[4,512,2,8,128]{4,3,2,1,0:T(8,128)} async-done(((f32[1,512,2,8,128]{4,3,2,1,0:T(8,128)}), f32[4,512,2,8,128]{4,3,2,1,0:T(8,128)}) %all-gather.10.cloned.1.call-update) | async-done | bytes 16777232 | tf_op jit(solution)/shard_map/all_gather | solution.py:26
  447.2 11.6 %fusion.47 = f32[1,512,2,8,128]{4,3,2,1,0:T(8,128)} fusion(f32[4,512,2,8,128]{4,3,2,1,0:T(8,128)} %all-gather.10.cloned.1.call-done, f32[512,2,8]{2,1,0:T(2,128)} %copy.78, f32[512,2,8]{2,1,0:T(2,128)} %copy.77, f32[512,2,8]{2,1,0:T(2,128)} %copy.76, f32[512,2,8]{2,1,0:T(2,128)} %copy.75, f32[512,2,8]{2,1,0:T(2,128)} %copy.74, f32[512,2,8]{2,1,0:T(2,128)} %copy.73), kind=kLoop, calls=%fused_computation.62 | loop fusion | flops 9437184 | bytes 21168128 | tf_op jit(solution)/shard_map/add | solution.py:129
  466.8 9.4 all_gather.52
  476.2 11.5 %all_gather.49 = f32[4,512,2,8]{1,3,2,0:T(8,128)S(1)} all-gather(f32[1,512,2,8]{1,3,2,0:T(8,128)S(1)} %get-tuple-element.319), channel_id=1, replica_groups=mesh['video_0'=2,'video_1'=4,'video_2'=4,'head'=4] {'video_2'}, dimensions={0}, use_global_device_ids=true | all-gather | bytes 163840 | tf_op jit(solution)/shard_map/all_gather | solution.py:26
  487.6 11.0 %all_gather.53 = f32[4,512,2,8]{1,3,2,0:T(8,128)S(1)} all-gather(f32[1,512,2,8]{1,3,2,0:T(8,128)S(1)} %get-tuple-element.318), channel_id=1, replica_groups=mesh['video_0'=2,'video_1'=4,'video_2'=4,'head'=4] {'video_2'}, dimensions={0}, use_global_device_ids=true | all-gather | bytes 163840 | tf_op jit(solution)/shard_map/all_gather | solution.py:26
  499.4 116.7 %all-gather.12.cloned.1.call-done = f32[4,512,2,8,128]{4,3,2,1,0:T(8,128)} async-done(((f32[1,512,2,8,128]{4,3,2,1,0:T(8,128)}), f32[4,512,2,8,128]{4,3,2,1,0:T(8,128)}) %all-gather.12.cloned.1.call-update) | async-done | bytes 16777232 | tf_op jit(solution)/shard_map/all_gather | solution.py:26
  616.1 12.2 %fusion.97 = (f32[1,512,2,8,128]{4,3,2,1,0:T(8,128)}, f32[1,512,2,8,128]{4,3,2,1,0:T(8,128)}, f32[1,512,2,8,128]{4,3,2,1,0:T(8,128)}, f32[1,512,2,8,128]{4,3,2,1,0:T(8,128)}) fusion(f32[4,512,2,8,128]{4,3,2,1,0:T(8,128)} %all-gather.12.cloned.1.call-done), kind=kLoop, calls=%fused_computation.174 | loop fusion | bytes 33554432 | tf_op jit(solution)/shard_map/slice | solution.py:27
  628.3 5.3 copy.106
  633.6 5.3 copy.107
  638.9 5.3 copy.108
  644.2 5.3 copy.109
  649.5 8.5 fusion.62
  658.0 64.7 %while.31 = (s32[]{:T(128)}, f32[512,2,8,128]{0,3,2,1:T(8,128)}, bf16[4,128,2,128]{3,1,2,0:T(8,128)(2,1)S(1)}, bf16[4,128,2,128]{3,1,2,0:T(8,128)(2,1)}, bf16[4,...) while((s32[]{:T(128)}, f32[512,2,8,128]{0,3,2,1:T(8,128)}, ...), condition=%wide.region_6.7_spmd.clone, body=%wide.region_5.6_spmd.clone.sunk | while | flops 1358004224 | bytes 95524192 | solution.py:67
  664.6 4.5 bitcast_add_fusion.5
  679.9 5.7 bitcast_add_fusion.5
  696.3 5.7 bitcast_add_fusion.5
  712.8 5.7 bitcast_add_fusion.5
  722.7 188.4 %all-reduce.1 = bf16[512,2,8,128]{0,3,2,1:T(8,128)(2,1)S(1)} all-reduce(f32[512,2,8,128]{0,3,2,1:T(8,128)} %get-tuple-element.120), channel_id=1, replica_groups=mesh['video_0'=2,'video_1'=4,'video_2'=4,'head'=4] {'video_0','video_1',..., use_global_device_ids=true, to_apply=%region_7.8 | all-reduce | flops 1048576 | bytes 6291456 | tf_op jit(solution)/shard_map/psum | solution.py:158
  920.5 31.1 %reduce-scatter.2.cloned.1.call-done = f32[128,256]{1,0:T(8,128)} async-done(((f32[512,256]{1,0:T(8,128)}), f32[128,256]{1,0:T(8,128)}) %reduce-scatter.2.cloned.1.call-update) | async-done | bytes 131088 | tf_op jit(solution)/shard_map/reduce_scatter | solution.py:165
  (176 shorter events, 117.8 us)
Async XLA Ops:
  7.2 904.0 %copy-start = (bf16[2048,256]{1,0:T(8,128)(2,1)S(1)}, bf16[2048,256]{1,0:T(8,128)(2,1)}, u32[]{:S(2)}) copy-start(bf16[2048,256]{1,0:T(8,128)(2,1)} %param.17) | copy-start | bytes 3145732
  7.2 88.7 %all-gather.8.cloned.1.call-start = ((), (), s32[]{:S(2)}) async-start(), calls=%async_computation.1 | async-start | bytes 4325376 | tf_op jit(solution)/shard_map/all_gather | solution.py:17
  8.9 276.9 %all-gather.14.cloned.1.call-start = ((), (), s32[]{:S(2)}) async-start(), calls=%async_computation.5 | async-start | bytes 12582912 | tf_op jit(solution)/shard_map/all_gather | solution.py:26
  100.0 5.6 copy-start.7
  179.0 268.2 %all-gather.10.cloned.1.call-start = ((), (), s32[]{:S(2)}) async-start(), calls=%async_computation.2 | async-start | bytes 20971520 | tf_op jit(solution)/shard_map/all_gather | solution.py:26
  293.7 322.4 %all-gather.12.cloned.1.call-start = ((), (), s32[]{:S(2)}) async-start(), calls=%async_computation.3 | async-start | bytes 20971520 | tf_op jit(solution)/shard_map/all_gather | solution.py:26
  458.8 492.9 %reduce-scatter.2.cloned.1.call-start = ((), (), s32[]{:S(2)}) async-start(), calls=%async_computation.4 | async-start | bytes 655360 | tf_op jit(solution)/shard_map/reduce_scatter | solution.py:165
  658.0 3.7 copy-start.4
  658.0 3.7 copy-start.8
  658.0 3.7 copy-start.9
  664.6 4.5 copy-start.1
  664.6 5.2 copy-start.5
  669.1 2.2 copy-start.3
  673.3 3.7 copy-start.4
  673.3 3.7 copy-start.8
  673.3 3.7 copy-start.9
  679.9 5.8 copy-start.1
  679.9 6.5 copy-start.5
  685.6 2.2 copy-start.3
  689.7 3.7 copy-start.4
  689.7 3.7 copy-start.8
  689.7 3.7 copy-start.9
  696.3 5.8 copy-start.1
  696.3 6.5 copy-start.5
  702.1 2.2 copy-start.3
  706.2 3.7 copy-start.4
  706.2 3.7 copy-start.8
  706.2 3.7 copy-start.9
  712.8 5.8 copy-start.1
  712.8 6.5 copy-start.5
  718.5 2.2 copy-start.3
  722.7 190.0 %copy-start.6 = (bf16[4,128,2,128]{3,1,2,0:T(8,128)(2,1)}, bf16[4,128,2,128]{3,1,2,0:T(8,128)(2,1)S(1)}, u32[]{:S(2)}) copy-start(bf16[4,128,2,128]{3,1,2,0:T(8,128)(2,1)S(1)} %get-tuple-element.121) | copy-start | bytes 786436
  (4 other events, 7.8 us)
Sparse Core Ops, SparseCore 0:
  11.7 84.1 all-gather.7
  179.1 106.5 all-gather.13
  293.9 153.2 all-gather.9
  458.9 157.1 all-gather.11
  912.8 38.8 reduce-scatter.1
where the time goes:
time: 962 us; the launch traced here: 960 us
  waiting for transfers between devices  460 us (48%)
  blocking collectives  240 us (25%)
  matrix products  103 us (11%)
  local copies, waits for them, and re-layouts  96.6 us (10%)
  other arithmetic  46.6 us (5%)
  between operations  13.9 us (1%)
    all_gather x3, waiting for transfers between devices, joined_all(): pieces = jax.tree.map(lambda part: lax.all_gather(part, axis), x)  349 us
    psum x1, blocking collectives, shards(): query_total = lax.psum(query_sum, VIDEO)  188 us
    all_gather x1, waiting for transfers between devices, side_by_side(): filled, at, outs = (lax.all_gather(both, axis, axis=dim, tiled=True), 0, [])  79.9 us
    all_gather x6, blocking collectives, joined_all(): pieces = jax.tree.map(lambda part: lax.all_gather(part, axis), x)  51.1 us
    unnamed x16, local copies, waits for them, and re-layouts  37.2 us
    dot_general x4, matrix products, block_step(): jnp.einsum('rgjk,kgd->rgjd', weights, value_block.astype(jnp.float32), pr...  35.5 us
    reduce_scatter x1, waiting for transfers between devices, shards(): lax.psum_scatter(partial_text, 'head', scatter_dimension=0, tiled=True)  31.1 us
    dot_general x4, matrix products, block_step(): jnp.einsum('rgjk,kgd->rgjd', score_grads, key_block, preferred_element_ty...  21.8 us
  transfers between devices with their start and end apart: 5, of which 5 were waited for; matrix products, arithmetic and copies ran while one was open for 3% of the time, Pallas kernels for 0%

commit v1 on v0

--- a/solution.py
+++ b/solution.py
@@ -155,7 +155,7 @@
     query_start = jnp.zeros(partial_value[2].shape, jnp.float32)
     block_step = backward_step(query_heads, grad_heads, query_frame, log_total, row_dots)
     query_sum, key_value = sweep(block_step, query_start, own_layout, zero_grads)
-    query_total = lax.psum(query_sum, VIDEO)
+    query_total = jnp.sum(lax.all_gather(query_sum, VIDEO), axis=0)
     query_grad_all = query_total.reshape(total_rows, -1).astype(jnp.bfloat16)
     query_grad = lax.dynamic_slice_in_dim(query_grad_all, video_index * query_rows, query_rows, 0)
     key_sum, value_sum = key_value

time: 962 us -> 1850 us (1.92)
  waiting for transfers between devices: 460 us -> 1420 us
  blocking collectives: 240 us -> 50.9 us
  local copies, waits for them, and re-layouts: 96.6 us -> 232 us
  matrix products: 103 us -> 53.3 us
  other arithmetic: 46.6 us -> 78.4 us
    all_gather x0 -> x1, waiting for transfers between devices: none -> 975 us  [shards(): query_total = jnp.sum(lax.all_gather(query_sum, VIDEO), axis=0)]
    psum x1 -> x0, blocking collectives: 188 us -> none  [shards(): query_total = lax.psum(query_sum, VIDEO)]
    unnamed x16 -> x19, local copies, waits for them, and re-layouts: 37.2 us -> 163 us
    reduce_sum x0 -> x1, other arithmetic: none -> 41.1 us  [shards(): query_total = jnp.sum(lax.all_gather(query_sum, VIDEO), axis=0)]
    reduce_scatter x1, waiting for transfers between devices: 31.1 us -> 11.6 us  [shards(): lax.psum_scatter(partial_text, 'head', scatter_dimension=0, tiled=True)]
  transfers between devices with their start and end apart: 5 -> 6, of which waited for: 5 -> 6; matrix products, arithmetic and copies ran while one was open for 3% -> 2% of each run, Pallas kernels for 0% -> 0%
where the time goes in v1:
time: 1850 us
  waiting for transfers between devices  1420 us (77%)
  local copies, waits for them, and re-layouts  232 us (13%)
  other arithmetic  78.4 us (4%)
  matrix products  53.3 us (3%)
  blocking collectives  50.9 us (3%)
    all_gather x1, waiting for transfers between devices, shards(): query_total = jnp.sum(lax.all_gather(query_sum, VIDEO), axis=0)  975 us
    all_gather x3, waiting for transfers between devices, joined_all(): pieces = jax.tree.map(lambda part: lax.all_gather(part, axis), x)  349 us
    unnamed x19, local copies, waits for them, and re-layouts  163 us
    all_gather x1, waiting for transfers between devices, side_by_side(): filled, at, outs = (lax.all_gather(both, axis, axis=dim, tiled=True), 0, [])  79.9 us
    all_gather x6, blocking collectives, joined_all(): pieces = jax.tree.map(lambda part: lax.all_gather(part, axis), x)  50.9 us
    reduce_sum x1, other arithmetic, shards(): query_total = jnp.sum(lax.all_gather(query_sum, VIDEO), axis=0)  41.1 us
  transfers between devices with their start and end apart: 6, of which 6 were waited for; matrix products, arithmetic and copies ran while one was open for 2% of the time, Pallas kernels for 0%

profile of v1, /device:TPU:1, one launch (start us, length us, event | category | flops | bytes accessed | tf_op | source)
XLA Modules:
  0.0 1846.7 jit_solution(8263728899949590704)
XLA Ops:
  16.0 79.9 %all-gather.10.cloned.1.call-done = bf16[512,4096]{1,0:T(8,128)(2,1)} async-done(((bf16[16,4096]{1,0:T(8,128)(2,1)}), bf16[512,4096]{1,0:T(8,128)(2,1)}) %all-gather.10.cloned.1.call-update) | async-done | bytes 4194320 | tf_op jit(solution)/shard_map/all_gather | solution.py:17
  95.8 4.2 fusion.98
  105.6 44.5 %while.30 = (s32[]{:T(128)}, f32[512,2,8]{0,2,1:T(8,128)S(1)}, f32[512,2,8]{0,2,1:T(8,128)S(1)}, f32[512,2,8,128]{0,3,2,1:T(8,128)}, s32[4,128]{1,0:T(4,128)S(1)...) while((s32[]{:T(128)}, f32[512,2,8]{0,2,1:T(8,128)S(1)}, ...), condition=%wide.region_3.4_spmd.clone, body=%wide.region_0.0_spmd.clone.sunk | while | flops 1894883328 | bytes 57806532 | solution.py:67
  109.7 5.0 bitcast_add_fusion.4
  120.9 5.0 bitcast_add_fusion.4
  132.0 5.0 bitcast_add_fusion.4
  143.1 5.0 bitcast_add_fusion.4
  150.1 5.5 copy.68
  155.6 4.9 all-gather
  162.6 99.7 %all-gather.16.cloned.1.call-done = f32[1024,2,8,128]{3,2,1,0:T(8,128)} async-done(((f32[512,2,8,128]{3,2,1,0:T(8,128)}), f32[1024,2,8,128]{3,2,1,0:T(8,128)}) %all-gather.16.cloned.1.call-update) | async-done | bytes 8388624 | tf_op jit(solution)/shard_map/all_gather | solution.py:26
  262.3 8.0 fusion.53
  270.4 4.9 all-gather.1
  275.3 9.6 all_gather.54
  291.2 132.6 %all-gather.12.cloned.1.call-done = f32[4,512,2,8,128]{4,3,2,1,0:T(8,128)} async-done(((f32[1,512,2,8,128]{4,3,2,1,0:T(8,128)}), f32[4,512,2,8,128]{4,3,2,1,0:T(8,128)}) %all-gather.12.cloned.1.call-update) | async-done | bytes 16777232 | tf_op jit(solution)/shard_map/all_gather | solution.py:26
  423.8 11.6 fusion.47
  435.4 4.0 copy.102
  439.4 4.0 copy.84
  443.4 9.2 all_gather.58
  452.6 11.5 all_gather.59
  464.0 10.8 all_gather.55
  475.6 117.1 %all-gather.14.cloned.1.call-done = f32[4,512,2,8,128]{4,3,2,1,0:T(8,128)} async-done(((f32[1,512,2,8,128]{4,3,2,1,0:T(8,128)}), f32[4,512,2,8,128]{4,3,2,1,0:T(8,128)}) %all-gather.14.cloned.1.call-update) | async-done | bytes 16777232 | tf_op jit(solution)/shard_map/all_gather | solution.py:26
  592.7 12.2 fusion.97
  604.9 5.3 copy.103
  610.2 5.4 copy.105
  615.6 5.3 copy.104
  620.8 5.3 copy.106
  626.1 8.6 fusion.62
  634.7 43.1 %while.31 = (s32[]{:T(128)}, f32[512,2,8,128]{0,3,2,1:T(8,128)}, bf16[4,128,2,128]{3,1,2,0:T(8,128)(2,1)}, bf16[4,128,2,128]{3,1,2,0:T(8,128)(2,1)}, bf16[4,128,...) while((s32[]{:T(128)}, f32[512,2,8,128]{0,3,2,1:T(8,128)}, ...), condition=%wide.region_6.7_spmd.clone, body=%wide.region_5.6_spmd.clone.sunk | while | flops 1358004224 | bytes 82939824 | solution.py:67
  678.1 975.0 %all-gather.18.cloned.1.call-done = f32[16384,2,8,128]{0,3,2,1:T(8,128)} async-done(((f32[512,2,8,128]{0,3,2,1:T(8,128)}), f32[16384,2,8,128]{0,3,2,1:T(8,128)}) %all-gather.18.cloned.1.call-update) | async-done | bytes 134217744 | tf_op jit(solution)/shard_map/all_gather | solution.py:158
  1653.1 125.7 %copy.108 = f32[256,8,32,512]{3,2,1,0:T(8,128)} copy(f32[256,8,32,512]{3,1,2,0:T(8,128)} %bitcast.68) | data formatting | bytes 268435456
  1778.8 41.1 %reduce_sum.28 = bf16[512,2,8,128]{0,3,2,1:T(8,128)(2,1)S(1)} reduce(f32[32,512,2,8,128]{1,0,4,3,2:T(8,128)} %bitcast.71, f32[]{:T(128)} %constant.84.clone.1), dimensions={0}, to_apply=%region_7.8 | reduce | flops 32505856 | bytes 136314880 | tf_op jit(solution)/shard_map/reduce_sum | solution.py:158
  1826.7 11.6 reduce-scatter.2.cloned.1.call-done
  (214 shorter events, 98.8 us)
Async XLA Ops:
  7.2 1812.7 %copy-start = (bf16[2048,256]{1,0:T(8,128)(2,1)S(1)}, bf16[2048,256]{1,0:T(8,128)(2,1)}, u32[]{:S(2)}) copy-start(bf16[2048,256]{1,0:T(8,128)(2,1)} %param.17) | copy-start | bytes 3145732
  7.2 88.7 %all-gather.10.cloned.1.call-start = ((), (), s32[]{:S(2)}) async-start(), calls=%async_computation.1 | async-start | bytes 4325376 | tf_op jit(solution)/shard_map/all_gather | solution.py:17
  8.9 253.4 %all-gather.16.cloned.1.call-start = ((), (), s32[]{:S(2)}) async-start(), calls=%async_computation.5 | async-start | bytes 12582912 | tf_op jit(solution)/shard_map/all_gather | solution.py:26
  100.0 5.6 copy-start.12
  106.8 3.0 copy-start.3
  114.8 2.0 copy-start.4
  117.9 3.0 copy-start.3
  125.9 2.0 copy-start.4
  129.0 3.0 copy-start.3
  137.0 2.0 copy-start.4
  140.1 3.0 copy-start.3
  148.1 2.0 copy-start.4
  155.6 268.2 %all-gather.12.cloned.1.call-start = ((), (), s32[]{:S(2)}) async-start(), calls=%async_computation.2 | async-start | bytes 20971520 | tf_op jit(solution)/shard_map/all_gather | solution.py:26
  270.3 322.4 %all-gather.14.cloned.1.call-start = ((), (), s32[]{:S(2)}) async-start(), calls=%async_computation.3 | async-start | bytes 20971520 | tf_op jit(solution)/shard_map/all_gather | solution.py:26
  435.4 1217.7 %all-gather.18.cloned.1.call-start = ((), (), s32[]{:S(2)}) async-start(), calls=%async_computation.6 | async-start | bytes 138412032 | tf_op jit(solution)/shard_map/all_gather | solution.py:158
  626.1 8.6 copy-start.5
  634.7 1.9 copy-start.6
  634.7 1.9 copy-start.7
  639.5 2.2 copy-start.1
  643.5 2.0 copy-start.2
  645.5 1.9 copy-start.6
  645.5 1.9 copy-start.7
  650.3 2.2 copy-start.1
  654.3 2.0 copy-start.2
  656.3 1.9 copy-start.7
  661.1 2.2 copy-start.1
  665.1 2.0 copy-start.2
  667.0 1.9 copy-start.6
  667.0 1.9 copy-start.7
  671.9 2.2 copy-start.1
  675.9 2.0 copy-start.2
  677.8 1160.4 %reduce-scatter.2.cloned.1.call-start = ((), (), s32[]{:S(2)}) async-start(), calls=%async_computation.4 | async-start | bytes 655360 | tf_op jit(solution)/shard_map/reduce_scatter | solution.py:165
  (22 other events, 36.3 us)
Sparse Core Ops, SparseCore 0:
  11.7 84.1 all-gather.9
  155.7 106.5 all-gather.15
  270.4 153.2 all-gather.11
  435.5 157.1 all-gather.13
  678.0 975.0 all-gather.17
  1821.6 16.6 reduce-scatter.1
